TPU v7x, 128 devices: a whole 4x4x4 slice. The times are simulated.
128 devices in a mesh: seq: 16 (over z, x), hid: 4 (over y), rep: 2 (over core).
Axes of the slice: x: 4, y: 4, z: 4, core: 2. Of those that a mesh axis runs over, the one named last changes fastest.
Arguments:
- tokens: bfloat16 [16384, 5376], P(('rep', 'seq'), 'hid'), parts along dimension 0, may hold values from -6 to 6
- norm_gain: float32 [5376], replicated, may hold values from 0.1 to 1.9
- w_query: bfloat16 [5376, 4096], P('seq', 'hid'), may hold values from -0.078125 to 0.078125
- w_key: bfloat16 [5376, 2048], P('seq', 'hid'), may hold values from -0.078125 to 0.078125
- w_value: bfloat16 [5376, 2048], P('seq', 'hid'), may hold values from -0.078125 to 0.078125
- query_gain: float32 [128], replicated, may hold values from 0.5 to 8
- key_gain: float32 [128], replicated, may hold values from 0.5 to 8
- w_out: bfloat16 [4096, 5376], P('hid', 'seq'), may hold values from -0.09375 to 0.09375
Outputs:
- attended: bfloat16 [16384, 5376], P(('rep', 'seq'), 'hid'), parts along dimension 0
There are 2 independent parts, one for each index of `rep`. A program takes and returns all parts, laid end to end along the dimension named above; an argument that names none is the same for every part. Nothing has to cross between parts.
All inputs are finite; a program needn't handle non-finite values.
Results may differ from a plain program's by a relative error of at most 0.023.
The roundings to bfloat16 on the way count: a program that leaves them out, or rounds other values in their place, can miss the bound.
Values may be sent and summed in bfloat16 or wider, within the bound.
A program may use at most 128 MiB of HBM per device.

v0:
```python
import jax
import jax.numpy as jnp
from jax import lax
from jax.sharding import PartitionSpec as P

HEAD_WIDTH = 128
WINDOW = 1024
QSCALE = 168
DEPTH = 2


def shifted(x, axis, by):
    count = lax.axis_size(axis)
    pairs = [(i, i + by) for i in range(count) if 0 <= i + by < count]
    return lax.ppermute(x, axis, pairs)


def rope(heads, positions):
    half = heads.shape[-1] // 2
    freq = 10000.0 ** (-(jnp.arange(half, dtype=jnp.float32) * 2.0) / heads.shape[-1])
    angle = positions[:, None] * freq[None, :]
    cosine = jnp.cos(angle)[:, None, :]
    sine = jnp.sin(angle)[:, None, :]
    first = heads[..., :half]
    second = heads[..., half:]
    return jnp.concatenate(
        [first * cosine - second * sine, second * cosine + first * sine], axis=-1
    )


def head_norm(heads, gain):
    return heads * lax.rsqrt(jnp.mean(heads * heads, axis=-1, keepdims=True) + 1e-06) * gain


def add_rows(normed, piece):
    return jnp.dot(normed, piece, preferred_element_type=jnp.float32)


def shards(tokens, norm_gain, w_query, w_key, w_value, query_gain, key_gain, w_out):
    whole = lax.all_gather(tokens, "hid", axis=1, tiled=True)
    xfloat = whole.astype(jnp.float32)
    normed = (
        xfloat * lax.rsqrt(jnp.mean(xfloat * xfloat, axis=-1, keepdims=True) + 1e-06) * norm_gain
    ).astype(jnp.bfloat16)
    rows = normed.shape[0]

    def add_one(piece):
        return add_rows(normed, piece)

    query = add_one(lax.all_gather(w_query, "seq", axis=0, tiled=True))
    key = add_one(lax.all_gather(w_key, "seq", axis=0, tiled=True))
    value = add_one(lax.all_gather(w_value, "seq", axis=0, tiled=True))
    local_heads = w_query.shape[1] // HEAD_WIDTH
    local_kv = w_key.shape[1] // HEAD_WIDTH
    base = lax.axis_index("seq") * rows
    qpos = base + jnp.arange(rows, dtype=jnp.int32)
    positions = qpos.astype(jnp.float32)
    qh = (
        rope(head_norm(query.reshape(rows, local_heads, HEAD_WIDTH), query_gain), positions)
        * QSCALE ** (-0.5)
    ).astype(jnp.bfloat16)
    kh = rope(head_norm(key.reshape(rows, local_kv, HEAD_WIDTH), key_gain), positions).astype(
        jnp.bfloat16
    )
    value_head = value.reshape(rows, local_kv, HEAD_WIDTH).astype(jnp.bfloat16)
    key_blocks = []
    value_blocks = []
    for distance in range(1, DEPTH + 1):
        arrived = shifted((kh, value_head), "seq", distance)
        key_blocks.insert(0, arrived[0])
        value_blocks.insert(0, arrived[1])
    keys = jnp.concatenate(key_blocks + [kh], axis=0)
    values = jnp.concatenate(value_blocks + [value_head], axis=0)
    window_extent = keys.shape[0]
    kpos = base - DEPTH * rows + jnp.arange(window_extent, dtype=jnp.int32)
    diff = qpos[:, None] - kpos[None, :]
    allowed = (diff >= 0) & (diff < WINDOW) & (kpos >= 0)[None, :]
    group = local_heads // local_kv
    grouped = qh.reshape(rows, local_kv, group, HEAD_WIDTH).transpose(1, 0, 2, 3)

    def one_head(operands):
        qpart, kpart, vpart = operands
        scores = jnp.einsum("rgd,ld->grl", qpart, kpart, preferred_element_type=jnp.float32)
        scores = jnp.where(allowed[None], scores, -jnp.inf)
        probs = jax.nn.softmax(scores, axis=-1).astype(jnp.bfloat16)
        mixed = jnp.einsum("grl,ld->rgd", probs, vpart, preferred_element_type=jnp.float32)
        return mixed.astype(jnp.bfloat16)

    per_head = lax.map(one_head, (grouped, keys.transpose(1, 0, 2), values.transpose(1, 0, 2)))
    heads_out = per_head.transpose(1, 0, 2, 3).reshape(rows, local_heads * HEAD_WIDTH)
    terms = jnp.dot(
        heads_out,
        lax.all_gather(w_out, "seq", axis=1, tiled=True),
        preferred_element_type=jnp.float32,
    )
    return lax.psum_scatter(terms.astype(jnp.bfloat16), "hid", scatter_dimension=1, tiled=True)


def solution(mesh):
    return jax.shard_map(
        shards,
        mesh=mesh,
        in_specs=(
            P(("rep", "seq"), "hid"),
            P(),
            P("seq", "hid"),
            P("seq", "hid"),
            P("seq", "hid"),
            P(),
            P(),
            P("hid", "seq"),
        ),
        out_specs=P(("rep", "seq"), "hid"),
        check_vma=False,
    )
```

profile of v0, /device:TPU:1, one launch (start us, length us, event | category | flops | bytes accessed | tf_op | source)
XLA Modules:
  0.0 466.9 jit_solution(10605443407271170900)
XLA Ops:
  11.0 60.4 %all-gather.6.cloned.1.call-done = bf16[512,5376]{0,1:T(8,128)(2,1)} async-done(((bf16[512,1344]{0,1:T(8,128)(2,1)}), bf16[512,5376]{0,1:T(8,128)(2,1)}) %all-gather.6.cloned.1.call-update) | async-done | bytes 5505040 | tf_op jit(solution)/shard_map/all_gather | solution.py:40
  71.4 3.8 fusion.41
  75.2 56.7 %all-gather.10.cloned.1.call-done = bf16[5376,512]{1,0:T(8,128)(2,1)} async-done(((bf16[336,512]{1,0:T(8,128)(2,1)}), bf16[5376,512]{1,0:T(8,128)(2,1)}) %all-gather.10.cloned.1.call-update) | async-done | bytes 5505040 | tf_op jit(solution)/shard_map/all_gather | solution.py:51
  131.9 7.6 %multiply_reduce_fusion.1 = (f32[512,4]{0,1:T(4,128)S(1)}, f32[512,512]{0,1:T(8,128)S(1)}) fusion(bf16[5376,512]{1,0:T(8,128)(2,1)} %all-gather.10.cloned.1.call-done, bf16[512,5376]{0,1:T(8,128)(2,1)} %all-gather.6.cloned.1.call-done, f32[5376]{0:T(1024)S(1)} %copy-done.2, f32[512]{0:T(512)S(1)} %add_rsqrt_fusion.2), kind=kOutput, calls=%fused_computation.52 | convolution fusion | flops 2830104576 | bytes 12090368 | tf_op jit(solution)/shard_map/dot_general | solution.py:36
  141.0 4.6 collective-permute-start.2
  147.9 54.8 %all-gather.8.cloned.1.call-done = bf16[5376,512]{1,0:T(8,128)(2,1)} async-done(((bf16[336,512]{1,0:T(8,128)(2,1)}), bf16[5376,512]{1,0:T(8,128)(2,1)}) %all-gather.8.cloned.1.call-update) | async-done | bytes 5505040 | tf_op jit(solution)/shard_map/all_gather | solution.py:52
  202.7 8.4 %convolution_convert_fusion.1 = bf16[512,512]{0,1:T(8,128)(2,1)} fusion(bf16[5376,512]{1,0:T(8,128)(2,1)} %all-gather.8.cloned.1.call-done, bf16[512,5376]{0,1:T(8,128)(2,1)} %all-gather.6.cloned.1.call-done, f32[5376]{0:T(1024)S(1)} %copy-done.2, f32[512]{0:T(512)S(1)} %add_rsqrt_fusion.2), kind=kOutput, calls=%fused_computation.47 | convolution fusion | flops 2829844480 | bytes 11557888 | tf_op jit(solution)/shard_map/dot_general | solution.py:36
  211.1 5.4 %collective-permute-start = (bf16[512,4,128]{0,2,1:T(8,128)(2,1)}, bf16[512,4,128]{0,2,1:T(8,128)(2,1)}, u32[]{:S(2)}, u32[]{:S(2)}) collective-permute-start(bf16[512,4,128]{0,2,1:T(8,128)(2,1)} %bitcast), channel_id=1, source_target_pairs={{0,16},{8,24},{16,32},{24,40},{32,48},{40,56},{48,64},{56,72},{64,... | collective-permute-start | bytes 1572872 | tf_op jit(solution)/shard_map/ppermute | solution.py:15
  221.1 12.3 %collective-permute-done = bf16[512,4,128]{0,2,1:T(8,128)(2,1)} collective-permute-done((bf16[512,4,128]{0,2,1:T(8,128)(2,1)}, bf16[512,4,128]{0,2,1:T(8,128)(2,1)}, u32[]{:S(2)}, u32[]{:S(2)}) %collective-permute-start) | collective-permute-done | bytes 524320 | tf_op jit(solution)/shard_map/ppermute | solution.py:15
  233.4 15.0 %collective-permute-done.1 = bf16[512,4,128]{0,2,1:T(8,128)(2,1)} collective-permute-done((bf16[512,4,128]{0,2,1:T(8,128)(2,1)}, bf16[512,4,128]{0,2,1:T(8,128)(2,1)}, u32[]{:S(2)}, u32[]{:S(2)}) %collective-permute-start.1) | collective-permute-done | bytes 524320 | tf_op jit(solution)/shard_map/ppermute | solution.py:15
  251.0 55.3 %all-gather.12.cloned.1.call-done = bf16[5376,1024]{1,0:T(8,128)(2,1)} async-done(((bf16[336,1024]{1,0:T(8,128)(2,1)}), bf16[5376,1024]{1,0:T(8,128)(2,1)}) %all-gather.12.cloned.1.call-update) | async-done | bytes 11010064 | tf_op jit(solution)/shard_map/all_gather | solution.py:50
  306.4 11.7 %convolution_bitcast_fusion = f32[64,8,8,128]{3,1,2,0:T(8,128)S(1)} fusion(bf16[5376,1024]{1,0:T(8,128)(2,1)} %all-gather.12.cloned.1.call-done, bf16[512,5376]{0,1:T(8,128)(2,1)} %all-gather.6.cloned.1.call-done, f32[5376]{0:T(1024)S(1)} %copy-done.2, f32[512]{0:T(512)S(1)} %add_rsqrt_fusion.2), kind=kOutput, calls=%fused_computation.44 | convolution fusion | flops 5648154624 | bytes 18635776 | tf_op jit(solution)/shard_map/dot_general | solution.py:36
  323.6 43.2 %while.11 = (s32[]{:T(128)}, bf16[4,512,2,128]{1,3,2,0:T(8,128)(2,1)S(1)}, bf16[4,1536,128]{1,2,0:T(8,128)(2,1)}, bf16[4,1536,128]{2,1,0:T(8,128)(2,1)}, bf16[4,...) while((s32[]{:T(128)}, ...), condition=%wide.region_6.7_spmd.clone, body=%wide.region_3.6_spmd.clone.sunk | while | flops 817235456 | bytes 15486557 | solution.py:89
  324.8 5.8 %fusion.75 = (f32[2,512]{1,0:T(2,128)S(1)}, f32[2,512,1536]{1,2,0:T(8,128)}) fusion(pred[512,1536]{0,1:T(8,128)(4,1)S(1)} %fusion.74, bf16[4,1536,128]{2,1,0:T(8,128)(2,1)} %get-tuple-element.159, s32[]{:T(128)} %get-tuple-element.147, bf16[4,512,2,128]{3,1,2,0:T(8,128)(2,1)S(1)} %get-tuple-element.160), kind=kOutput, calls=%fused_computation.65.clone.1 | convolution fusion | flops 407373312 | bytes 7738368 | tf_op jit(solution)/shard_map/while/body/eval_jaxpr/sub | solution.py:85
  330.6 3.6 fusion.76
  335.4 5.8 %fusion.75 = (f32[2,512]{1,0:T(2,128)S(1)}, f32[2,512,1536]{1,2,0:T(8,128)}) fusion(pred[512,1536]{0,1:T(8,128)(4,1)S(1)} %fusion.74, bf16[4,1536,128]{2,1,0:T(8,128)(2,1)} %get-tuple-element.159, s32[]{:T(128)} %get-tuple-element.147, bf16[4,512,2,128]{3,1,2,0:T(8,128)(2,1)S(1)} %get-tuple-element.160), kind=kOutput, calls=%fused_computation.65.clone.1 | convolution fusion | flops 407373312 | bytes 7738368 | tf_op jit(solution)/shard_map/while/body/eval_jaxpr/sub | solution.py:85
  341.2 4.3 fusion.76
  346.8 5.8 %fusion.75 = (f32[2,512]{1,0:T(2,128)S(1)}, f32[2,512,1536]{1,2,0:T(8,128)}) fusion(pred[512,1536]{0,1:T(8,128)(4,1)S(1)} %fusion.74, bf16[4,1536,128]{2,1,0:T(8,128)(2,1)} %get-tuple-element.159, s32[]{:T(128)} %get-tuple-element.147, bf16[4,512,2,128]{3,1,2,0:T(8,128)(2,1)S(1)} %get-tuple-element.160), kind=kOutput, calls=%fused_computation.65.clone.1 | convolution fusion | flops 407373312 | bytes 7738368 | tf_op jit(solution)/shard_map/while/body/eval_jaxpr/sub | solution.py:85
  352.6 3.6 fusion.76
  357.4 5.8 %fusion.75 = (f32[2,512]{1,0:T(2,128)S(1)}, f32[2,512,1536]{1,2,0:T(8,128)}) fusion(pred[512,1536]{0,1:T(8,128)(4,1)S(1)} %fusion.74, bf16[4,1536,128]{2,1,0:T(8,128)(2,1)} %get-tuple-element.159, s32[]{:T(128)} %get-tuple-element.147, bf16[4,512,2,128]{3,1,2,0:T(8,128)(2,1)S(1)} %get-tuple-element.160), kind=kOutput, calls=%fused_computation.65.clone.1 | convolution fusion | flops 407373312 | bytes 7738368 | tf_op jit(solution)/shard_map/while/body/eval_jaxpr/sub | solution.py:85
  363.2 3.5 fusion.76
  366.8 24.1 %all-gather.14.cloned.1.call-done = bf16[1024,5376]{0,1:T(8,128)(2,1)} async-done(((bf16[1024,336]{0,1:T(8,128)(2,1)}), bf16[1024,5376]{0,1:T(8,128)(2,1)}) %all-gather.14.cloned.1.call-update) | async-done | bytes 11010064 | tf_op jit(solution)/shard_map/all_gather | solution.py:93
  390.9 11.8 %convolution_convert_fusion = bf16[512,5376]{0,1:T(8,128)(2,1)} fusion(bf16[1024,5376]{0,1:T(8,128)(2,1)} %all-gather.14.cloned.1.call-done, bf16[512,1024]{0,1:T(8,128)(2,1)S(1)} %bitcast.83), kind=kOutput, calls=%fused_computation.37 | convolution fusion | flops 5639897088 | bytes 17563648 | tf_op jit(solution)/shard_map/dot_general | solution.py:91
  402.7 57.3 %reduce-scatter.2.cloned.1.call-done = bf16[512,1344]{0,1:T(8,128)(2,1)} async-done(((bf16[512,5376]{0,1:T(8,128)(2,1)}), bf16[512,1344]{0,1:T(8,128)(2,1)}) %reduce-scatter.2.cloned.1.call-update) | async-done | bytes 1376272 | tf_op jit(solution)/shard_map/reduce_scatter | solution.py:96
  (53 shorter events, 25.4 us)
Async XLA Ops:
  6.5 64.9 %all-gather.6.cloned.1.call-start = ((), (), s32[]{:S(2)}) async-start(), calls=%async_computation.1 | async-start | bytes 6881280 | tf_op jit(solution)/shard_map/all_gather | solution.py:40
  7.3 124.7 %all-gather.10.cloned.1.call-start = ((), (), s32[]{:S(2)}) async-start(), calls=%async_computation.3 | async-start | bytes 5849088 | tf_op jit(solution)/shard_map/all_gather | solution.py:51
  8.0 194.7 %all-gather.8.cloned.1.call-start = ((), (), s32[]{:S(2)}) async-start(), calls=%async_computation.2 | async-start | bytes 5849088 | tf_op jit(solution)/shard_map/all_gather | solution.py:52
  8.7 297.6 %all-gather.12.cloned.1.call-start = ((), (), s32[]{:S(2)}) async-start(), calls=%async_computation.4 | async-start | bytes 11698176 | tf_op jit(solution)/shard_map/all_gather | solution.py:50
  9.3 381.6 %all-gather.14.cloned.1.call-start = ((), (), s32[]{:S(2)}) async-start(), calls=%async_computation.5 | async-start | bytes 11698176 | tf_op jit(solution)/shard_map/all_gather | solution.py:93
  9.9 122.0 %copy-start.2 = (f32[5376]{0:T(1024)S(1)}, f32[5376]{0:T(1024)}, u32[]{:S(2)}) copy-start(f32[5376]{0:T(1024)} %param.11) | copy-start | bytes 64516
  9.9 450.1 %reduce-scatter.2.cloned.1.call-start = ((), (), s32[]{:S(2)}) async-start(), calls=%async_computation.6 | async-start | bytes 6881280 | tf_op jit(solution)/shard_map/reduce_scatter | solution.py:96
  75.2 64.7 %copy-start = (f32[128]{0:T(128)S(1)}, f32[128]{0:T(128)}, u32[]{:S(2)}) copy-start(f32[128]{0:T(128)} %param.16) | copy-start | bytes 1540
  141.0 78.6 %collective-permute-start.2 = (bf16[512,4,128]{2,0,1:T(8,128)(2,1)S(1)}, bf16[512,4,128]{2,0,1:T(8,128)(2,1)S(1)}, u32[]{:S(2)}, u32[]{:S(2)}) collective-permute-start(bf16[512,4,128]{2,0,1:T(8,128)(2,1)S(1)} %pad_maximum_fusion), channel_id=1, source_target_pairs={{0,16},{8,24},{16,32},{24,40},{32,48},{40,56},{48,64},{56,72},{64,... | collective-permute-start | bytes 1572872 | tf_op jit(solution)/shard_map/ppermute | solution.py:15
  145.6 73.9 %collective-permute-start.3 = (bf16[512,4,128]{2,0,1:T(8,128)(2,1)S(1)}, bf16[512,4,128]{2,0,1:T(8,128)(2,1)S(1)}, u32[]{:S(2)}, u32[]{:S(2)}) collective-permute-start(bf16[512,4,128]{2,0,1:T(8,128)(2,1)S(1)} %pad_maximum_fusion), channel_id=1, source_target_pairs={{0,8},{8,16},{16,24},{24,32},{32,40},{40,48},{48,56},{56,64},{64,7... | collective-permute-start | bytes 1572872 | tf_op jit(solution)/shard_map/ppermute | solution.py:15
  211.1 22.3 %collective-permute-start = (bf16[512,4,128]{0,2,1:T(8,128)(2,1)}, bf16[512,4,128]{0,2,1:T(8,128)(2,1)}, u32[]{:S(2)}, u32[]{:S(2)}) collective-permute-start(bf16[512,4,128]{0,2,1:T(8,128)(2,1)} %bitcast), channel_id=1, source_target_pairs={{0,16},{8,24},{16,32},{24,40},{32,48},{40,56},{48,64},{56,72},{64,... | collective-permute-start | bytes 1572872 | tf_op jit(solution)/shard_map/ppermute | solution.py:15
  216.5 31.9 %collective-permute-start.1 = (bf16[512,4,128]{0,2,1:T(8,128)(2,1)}, bf16[512,4,128]{0,2,1:T(8,128)(2,1)}, u32[]{:S(2)}, u32[]{:S(2)}) collective-permute-start(bf16[512,4,128]{0,2,1:T(8,128)(2,1)} %bitcast), channel_id=1, source_target_pairs={{0,8},{8,16},{16,24},{24,32},{32,40},{40,48},{48,56},{56,64},{64,7... | collective-permute-start | bytes 1572872 | tf_op jit(solution)/shard_map/ppermute | solution.py:15
  318.1 1.4 copy-start.1
  322.3 1.2 copy-start.3
Sparse Core Ops, SparseCore 0:
  9.0 62.3 all-gather.5
  73.5 58.3 all-gather.9
  134.1 68.5 all-gather.7
  204.7 101.6 all-gather.11
  308.3 82.4 all-gather.13
  402.8 57.1 reduce-scatter.1
where the time goes:
time: 467 us
  waiting for transfers between devices  339 us (73%)
  matrix products  77.8 us (17%)
  other arithmetic  18.1 us (4%)
  starting transfers between devices  15.5 us (3%)
  between operations  13.7 us (3%)
    all_gather x1, waiting for transfers between devices, shards(): whole = lax.all_gather(tokens, 'hid', axis=1, tiled=True)  60.4 us
    reduce_scatter x1, waiting for transfers between devices, shards(): lax.psum_scatter(terms.astype(jnp.bfloat16), 'hid', scatter_dimension=1,...  57.3 us
    all_gather x1, waiting for transfers between devices, shards(): key = add_one(lax.all_gather(w_key, 'seq', axis=0, tiled=True))  56.7 us
    all_gather x1, waiting for transfers between devices, shards(): query = add_one(lax.all_gather(w_query, 'seq', axis=0, tiled=True))  55.3 us
    all_gather x1, waiting for transfers between devices, shards(): value = add_one(lax.all_gather(w_value, 'seq', axis=0, tiled=True))  54.8 us
    dot_general x3, matrix products, add_rows(): return jnp.dot(normed, piece, preferred_element_type=jnp.float32)  27.7 us
    ppermute x4, waiting for transfers between devices, shifted(): return lax.ppermute(x, axis, pairs)  27.4 us
    all_gather x1, waiting for transfers between devices, shards(): lax.all_gather(w_out, 'seq', axis=1, tiled=True)  24.1 us
  transfers between devices with their start and end apart: 10, of which 8 were waited for; matrix products, arithmetic and copies ran while one was open for 18% of the time, Pallas kernels for 0%

commit v1 on v0

--- a/solution.py
+++ b/solution.py
@@ -37,7 +37,13 @@
 
 
 def shards(tokens, norm_gain, w_query, w_key, w_value, query_gain, key_gain, w_out):
-    whole = lax.all_gather(tokens, "hid", axis=1, tiled=True)
+    size = lax.axis_size("hid")
+    block, shards_2 = (tokens, [tokens])
+    for _ in range(size - 1):
+        block = lax.ppermute(block, "hid", [(i_2, (i_2 + 1) % size) for i_2 in range(size)])
+        shards_2.insert(0, block)
+    flat = jnp.concatenate(shards_2, axis=1)
+    whole = jnp.roll(flat, (lax.axis_index("hid") + 1) * tokens.shape[1], axis=1)
     xfloat = whole.astype(jnp.float32)
     normed = (
         xfloat * lax.rsqrt(jnp.mean(xfloat * xfloat, axis=-1, keepdims=True) + 1e-06) * norm_gain

time: 467 us -> 394 us (0.84)
  waiting for transfers between devices: 339 us -> 252 us
  local copies, waits for them, and re-layouts: 2.44 us -> 12 us
    ppermute x0 -> x3, waiting for transfers between devices: none -> 92.9 us  [shards(): lax.ppermute(block, 'hid', [(i_2, (i_2 + 1) % size) for i_2 in range(size)])]
    all_gather x1 -> x0, waiting for transfers between devices: 60.4 us -> none  [shards(): whole = lax.all_gather(tokens, 'hid', axis=1, tiled=True)]
    all_gather x1, waiting for transfers between devices: 56.7 us -> 0.02 us  [shards(): key = add_one(lax.all_gather(w_key, 'seq', axis=0, tiled=True))]
    all_gather x1, waiting for transfers between devices: 54.8 us -> 0.02 us  [shards(): value = add_one(lax.all_gather(w_value, 'seq', axis=0, tiled=True))]
    unnamed x9 -> x18, local copies, waits for them, and re-layouts: 1.08 us -> 10.5 us
    all_gather x1, waiting for transfers between devices: 55.3 us -> 48 us  [shards(): query = add_one(lax.all_gather(w_query, 'seq', axis=0, tiled=True))]
  transfers between devices with their start and end apart: 10 -> 12, of which waited for: 8 -> 9; matrix products, arithmetic and copies ran while one was open for 18% -> 24% of each run, Pallas kernels for 0% -> 0%
where the time goes in v1:
time: 394 us
  waiting for transfers between devices  252 us (64%)
  matrix products  81.5 us (21%)
  starting transfers between devices  18.9 us (5%)
  other arithmetic  16.3 us (4%)
  between operations  13.4 us (3%)
  local copies, waits for them, and re-layouts  12 us (3%)
    ppermute x3, waiting for transfers between devices, shards(): lax.ppermute(block, 'hid', [(i_2, (i_2 + 1) % size) for i_2 in range(size)])  92.9 us
    reduce_scatter x1, waiting for transfers between devices, shards(): lax.psum_scatter(terms.astype(jnp.bfloat16), 'hid', scatter_dimension=1,...  57.3 us
    all_gather x1, waiting for transfers between devices, shards(): query = add_one(lax.all_gather(w_query, 'seq', axis=0, tiled=True))  48 us
    ppermute x4, waiting for transfers between devices, shifted(): return lax.ppermute(x, axis, pairs)  29.9 us
    dot_general x3, matrix products, add_rows(): return jnp.dot(normed, piece, preferred_element_type=jnp.float32)  29.6 us
    sub x4, matrix products, one_head(): probs = jax.nn.softmax(scores, axis=-1).astype(jnp.bfloat16)  23.3 us
    all_gather x1, waiting for transfers between devices, shards(): lax.all_gather(w_out, 'seq', axis=1, tiled=True)  20.8 us
    dot_general x4, matrix products, one_head(): jnp.einsum('grl,ld->rgd', probs, vpart, preferred_element_type=jnp.float32)  18.2 us
  transfers between devices with their start and end apart: 12, of which 9 were waited for; matrix products, arithmetic and copies ran while one was open for 24% of the time, Pallas kernels for 0%

profile of v1, /device:TPU:1, one launch (start us, length us, event | category | flops | bytes accessed | tf_op | source)
XLA Modules:
  0.0 393.8 jit_solution(3031363065526724523)
XLA Ops:
  11.6 31.4 %collective-permute-done = bf16[512,1344]{0,1:T(8,128)(2,1)S(1)} collective-permute-done((bf16[512,1344]{0,1:T(8,128)(2,1)}, bf16[512,1344]{0,1:T(8,128)(2,1)S(1)}, u32[]{:S(2)}, u32[]{:S(2)}) %collective-permute-start) | collective-permute-done | bytes 1376288 | tf_op jit(solution)/shard_map/ppermute | solution.py:43
  43.0 31.6 %collective-permute-done.1 = bf16[512,1344]{0,1:T(8,128)(2,1)} collective-permute-done((bf16[512,1344]{0,1:T(8,128)(2,1)S(1)}, bf16[512,1344]{0,1:T(8,128)(2,1)}, u32[]{:S(2)}, u32[]{:S(2)}) %collective-permute-start.1) | collective-permute-done | bytes 1376288 | tf_op jit(solution)/shard_map/ppermute | solution.py:43
  75.6 29.9 %collective-permute-done.2 = bf16[512,1344]{0,1:T(8,128)(2,1)} collective-permute-done((bf16[512,1344]{0,1:T(8,128)(2,1)}, bf16[512,1344]{0,1:T(8,128)(2,1)}, u32[]{:S(2)}, u32[]{:S(2)}) %collective-permute-start.2) | collective-permute-done | bytes 1376288 | tf_op jit(solution)/shard_map/ppermute | solution.py:43
  117.6 8.6 %multiply_reduce_fusion.1 = (f32[512,4]{0,1:T(4,128)S(1)}, f32[512,512]{0,1:T(8,128)S(1)}) fusion(bf16[5376,512]{1,0:T(8,128)(2,1)} %all-gather.7.cloned.1.call-done, f32[5376]{0:T(1024)S(1)} %copy-done.4, f32[512]{0:T(512)S(1)} %add_rsqrt_fusion.2, bf16[512,10752]{0,1:T(8,128)(2,1)} %copy-done.1, s32[]{:T(128)S(6)} %select_n.18), kind=kOutput, calls=%fused_computation.52 | convolution fusion | flops 2830104576 | bytes 12090372 | tf_op jit(solution)/shard_map/dot_general | solution.py:36
  127.7 4.4 %collective-permute-start.5 = (bf16[512,4,128]{2,0,1:T(8,128)(2,1)S(1)}, bf16[512,4,128]{2,0,1:T(8,128)(2,1)S(1)}, u32[]{:S(2)}, u32[]{:S(2)}) collective-permute-start(bf16[512,4,128]{2,0,1:T(8,128)(2,1)S(1)} %pad_maximum_fusion), channel_id=1, source_target_pairs={{0,16},{8,24},{16,32},{24,40},{32,48},{40,56},{48,64},{56,72},{64,... | collective-permute-start | bytes 1572872 | tf_op jit(solution)/shard_map/ppermute | solution.py:15
  134.5 9.2 %convolution_convert_fusion.1 = bf16[512,512]{0,1:T(8,128)(2,1)} fusion(bf16[5376,512]{1,0:T(8,128)(2,1)} %all-gather.5.cloned.1.call-done, f32[5376]{0:T(1024)S(1)} %copy-done.4, f32[512]{0:T(512)S(1)} %add_rsqrt_fusion.2, bf16[512,10752]{0,1:T(8,128)(2,1)} %copy-done.1, s32[]{:T(128)S(6)} %select_n.18), kind=kOutput, calls=%fused_computation.47 | convolution fusion | flops 2829844480 | bytes 11557892 | tf_op jit(solution)/shard_map/dot_general | solution.py:36
  143.7 5.8 %collective-permute-start.3 = (bf16[512,4,128]{0,2,1:T(8,128)(2,1)}, bf16[512,4,128]{0,2,1:T(8,128)(2,1)}, u32[]{:S(2)}, u32[]{:S(2)}) collective-permute-start(bf16[512,4,128]{0,2,1:T(8,128)(2,1)} %bitcast), channel_id=1, source_target_pairs={{0,16},{8,24},{16,32},{24,40},{32,48},{40,56},{48,64},{56,72},{64,... | collective-permute-start | bytes 1572872 | tf_op jit(solution)/shard_map/ppermute | solution.py:15
  153.5 5.2 %collective-permute-done.6 = bf16[512,4,128]{2,0,1:T(8,128)(2,1)S(1)} collective-permute-done((bf16[512,4,128]{2,0,1:T(8,128)(2,1)S(1)}, bf16[512,4,128]{2,0,1:T(8,128)(2,1)S(1)}, u32[]{:S(2)}, u32[]{:S(2)}) %collective-permute-start.6) | collective-permute-done | bytes 524320 | tf_op jit(solution)/shard_map/ppermute | solution.py:15
  160.2 13.5 %collective-permute-done.3 = bf16[512,4,128]{0,2,1:T(8,128)(2,1)} collective-permute-done((bf16[512,4,128]{0,2,1:T(8,128)(2,1)}, bf16[512,4,128]{0,2,1:T(8,128)(2,1)}, u32[]{:S(2)}, u32[]{:S(2)}) %collective-permute-start.3) | collective-permute-done | bytes 524320 | tf_op jit(solution)/shard_map/ppermute | solution.py:15
  173.7 11.2 %collective-permute-done.4 = bf16[512,4,128]{0,2,1:T(8,128)(2,1)} collective-permute-done((bf16[512,4,128]{0,2,1:T(8,128)(2,1)}, bf16[512,4,128]{0,2,1:T(8,128)(2,1)}, u32[]{:S(2)}, u32[]{:S(2)}) %collective-permute-start.4) | collective-permute-done | bytes 524320 | tf_op jit(solution)/shard_map/ppermute | solution.py:15
  187.5 48.0 %all-gather.9.cloned.1.call-done = bf16[5376,1024]{1,0:T(8,128)(2,1)} async-done(((bf16[336,1024]{1,0:T(8,128)(2,1)}), bf16[5376,1024]{1,0:T(8,128)(2,1)}) %all-gather.9.cloned.1.call-update) | async-done | bytes 11010064 | tf_op jit(solution)/shard_map/all_gather | solution.py:56
  235.5 11.8 %convolution_bitcast_fusion = f32[64,8,8,128]{3,1,2,0:T(8,128)S(1)} fusion(bf16[5376,1024]{1,0:T(8,128)(2,1)} %all-gather.9.cloned.1.call-done, f32[5376]{0:T(1024)S(1)} %copy-done.4, f32[512]{0:T(512)S(1)} %add_rsqrt_fusion.2, bf16[512,10752]{0,1:T(8,128)(2,1)} %copy-done.1, s32[]{:T(128)S(6)} %select_n.18), kind=kOutput, calls=%fused_computation.44 | convolution fusion | flops 5648154624 | bytes 18635780 | tf_op jit(solution)/shard_map/dot_general | solution.py:36
  252.3 46.3 %while.11 = (s32[]{:T(128)}, bf16[4,512,2,128]{1,3,2,0:T(8,128)(2,1)}, bf16[4,1536,128]{1,2,0:T(8,128)(2,1)}, bf16[4,1536,128]{2,1,0:T(8,128)(2,1)}, bf16[4,512,...) while((s32[]{:T(128)}, ...), condition=%wide.region_6.7_spmd.clone, body=%wide.region_3.6_spmd.clone.sunk | while | flops 817235456 | bytes 15486557 | solution.py:95
  253.6 5.8 %fusion.75 = (f32[2,512]{1,0:T(2,128)S(1)}, f32[2,512,1536]{1,2,0:T(8,128)}) fusion(pred[512,1536]{0,1:T(8,128)(4,1)S(1)} %fusion.74, bf16[4,1536,128]{2,1,0:T(8,128)(2,1)} %get-tuple-element.159, s32[]{:T(128)} %get-tuple-element.147, bf16[4,512,2,128]{3,1,2,0:T(8,128)(2,1)S(1)} %get-tuple-element.160), kind=kOutput, calls=%fused_computation.73.clone.1 | convolution fusion | flops 407373312 | bytes 7738368 | tf_op jit(solution)/shard_map/while/body/eval_jaxpr/sub | solution.py:91
  259.4 4.3 %fusion.76 = bf16[4,512,2,128]{1,3,2,0:T(8,128)(2,1)} fusion(bf16[4,512,2,128]{1,3,2,0:T(8,128)(2,1)} %get-tuple-element.148, s32[]{:T(128)} %get-tuple-element.147, f32[2,512,1536]{1,2,0:T(8,128)} %get-tuple-element.136, f32[2,512]{1,0:T(2,128)S(1)} %get-tuple-element.137, bf16[4,1536,128]{1,2,0:T(8,128)(2,1)} %get-tuple-element.158), kind=kOutput, calls=%fused_computation.15.clone.1 | convolution fusion | flops 405929984 | bytes 6951936 | tf_op jit(solution)/shard_map/while/body/eval_jaxpr/grl,ld->rgd/dot_general | solution.py:92
  264.9 5.8 %fusion.75 = (f32[2,512]{1,0:T(2,128)S(1)}, f32[2,512,1536]{1,2,0:T(8,128)}) fusion(pred[512,1536]{0,1:T(8,128)(4,1)S(1)} %fusion.74, bf16[4,1536,128]{2,1,0:T(8,128)(2,1)} %get-tuple-element.159, s32[]{:T(128)} %get-tuple-element.147, bf16[4,512,2,128]{3,1,2,0:T(8,128)(2,1)S(1)} %get-tuple-element.160), kind=kOutput, calls=%fused_computation.73.clone.1 | convolution fusion | flops 407373312 | bytes 7738368 | tf_op jit(solution)/shard_map/while/body/eval_jaxpr/sub | solution.py:91
  270.7 5.2 %fusion.76 = bf16[4,512,2,128]{1,3,2,0:T(8,128)(2,1)} fusion(bf16[4,512,2,128]{1,3,2,0:T(8,128)(2,1)} %get-tuple-element.148, s32[]{:T(128)} %get-tuple-element.147, f32[2,512,1536]{1,2,0:T(8,128)} %get-tuple-element.136, f32[2,512]{1,0:T(2,128)S(1)} %get-tuple-element.137, bf16[4,1536,128]{1,2,0:T(8,128)(2,1)} %get-tuple-element.158), kind=kOutput, calls=%fused_computation.15.clone.1 | convolution fusion | flops 405929984 | bytes 6951936 | tf_op jit(solution)/shard_map/while/body/eval_jaxpr/grl,ld->rgd/dot_general | solution.py:92
  277.0 5.8 %fusion.75 = (f32[2,512]{1,0:T(2,128)S(1)}, f32[2,512,1536]{1,2,0:T(8,128)}) fusion(pred[512,1536]{0,1:T(8,128)(4,1)S(1)} %fusion.74, bf16[4,1536,128]{2,1,0:T(8,128)(2,1)} %get-tuple-element.159, s32[]{:T(128)} %get-tuple-element.147, bf16[4,512,2,128]{3,1,2,0:T(8,128)(2,1)S(1)} %get-tuple-element.160), kind=kOutput, calls=%fused_computation.73.clone.1 | convolution fusion | flops 407373312 | bytes 7738368 | tf_op jit(solution)/shard_map/while/body/eval_jaxpr/sub | solution.py:91
  282.9 4.4 %fusion.76 = bf16[4,512,2,128]{1,3,2,0:T(8,128)(2,1)} fusion(bf16[4,512,2,128]{1,3,2,0:T(8,128)(2,1)} %get-tuple-element.148, s32[]{:T(128)} %get-tuple-element.147, f32[2,512,1536]{1,2,0:T(8,128)} %get-tuple-element.136, f32[2,512]{1,0:T(2,128)S(1)} %get-tuple-element.137, bf16[4,1536,128]{1,2,0:T(8,128)(2,1)} %get-tuple-element.158), kind=kOutput, calls=%fused_computation.15.clone.1 | convolution fusion | flops 405929984 | bytes 6951936 | tf_op jit(solution)/shard_map/while/body/eval_jaxpr/grl,ld->rgd/dot_general | solution.py:92
  288.5 5.8 %fusion.75 = (f32[2,512]{1,0:T(2,128)S(1)}, f32[2,512,1536]{1,2,0:T(8,128)}) fusion(pred[512,1536]{0,1:T(8,128)(4,1)S(1)} %fusion.74, bf16[4,1536,128]{2,1,0:T(8,128)(2,1)} %get-tuple-element.159, s32[]{:T(128)} %get-tuple-element.147, bf16[4,512,2,128]{3,1,2,0:T(8,128)(2,1)S(1)} %get-tuple-element.160), kind=kOutput, calls=%fused_computation.73.clone.1 | convolution fusion | flops 407373312 | bytes 7738368 | tf_op jit(solution)/shard_map/while/body/eval_jaxpr/sub | solution.py:91
  294.3 4.4 %fusion.76 = bf16[4,512,2,128]{1,3,2,0:T(8,128)(2,1)} fusion(bf16[4,512,2,128]{1,3,2,0:T(8,128)(2,1)} %get-tuple-element.148, s32[]{:T(128)} %get-tuple-element.147, f32[2,512,1536]{1,2,0:T(8,128)} %get-tuple-element.136, f32[2,512]{1,0:T(2,128)S(1)} %get-tuple-element.137, bf16[4,1536,128]{1,2,0:T(8,128)(2,1)} %get-tuple-element.158), kind=kOutput, calls=%fused_computation.15.clone.1 | convolution fusion | flops 405929984 | bytes 6951936 | tf_op jit(solution)/shard_map/while/body/eval_jaxpr/grl,ld->rgd/dot_general | solution.py:92
  298.6 20.8 %all-gather.11.cloned.1.call-done = bf16[1024,5376]{0,1:T(8,128)(2,1)} async-done(((bf16[1024,336]{0,1:T(8,128)(2,1)}), bf16[1024,5376]{0,1:T(8,128)(2,1)}) %all-gather.11.cloned.1.call-update) | async-done | bytes 11010064 | tf_op jit(solution)/shard_map/all_gather | solution.py:99
  319.5 10.4 %convolution_convert_fusion = bf16[512,5376]{0,1:T(8,128)(2,1)} fusion(bf16[1024,5376]{0,1:T(8,128)(2,1)} %all-gather.11.cloned.1.call-done, bf16[512,1024]{0,1:T(8,128)(2,1)} %bitcast.83), kind=kOutput, calls=%fused_computation.37 | convolution fusion | flops 5639897088 | bytes 17563648 | tf_op jit(solution)/shard_map/dot_general | solution.py:97
  329.9 57.3 %reduce-scatter.2.cloned.1.call-done = bf16[512,1344]{0,1:T(8,128)(2,1)} async-done(((bf16[512,5376]{0,1:T(8,128)(2,1)}), bf16[512,1344]{0,1:T(8,128)(2,1)}) %reduce-scatter.2.cloned.1.call-update) | async-done | bytes 1376272 | tf_op jit(solution)/shard_map/reduce_scatter | solution.py:102
  (66 shorter events, 39.7 us)
Async XLA Ops:
  6.5 101.9 %copy-start = (bf16[512,1344]{0,1:T(8,128)(2,1)S(1)}, bf16[512,1344]{0,1:T(8,128)(2,1)}, u32[]{:S(2)}) copy-start(bf16[512,1344]{0,1:T(8,128)(2,1)} %param.10) | copy-start | bytes 4128772
  6.5 111.1 %all-gather.7.cloned.1.call-start = ((), (), s32[]{:S(2)}) async-start(), calls=%async_computation.2 | async-start | bytes 5849088 | tf_op jit(solution)/shard_map/all_gather | solution.py:57
  7.3 127.3 %all-gather.5.cloned.1.call-start = ((), (), s32[]{:S(2)}) async-start(), calls=%async_computation.1 | async-start | bytes 5849088 | tf_op jit(solution)/shard_map/all_gather | solution.py:58
  8.0 227.5 %all-gather.9.cloned.1.call-start = ((), (), s32[]{:S(2)}) async-start(), calls=%async_computation.3 | async-start | bytes 11698176 | tf_op jit(solution)/shard_map/all_gather | solution.py:56
  8.7 310.7 %all-gather.11.cloned.1.call-start = ((), (), s32[]{:S(2)}) async-start(), calls=%async_computation.4 | async-start | bytes 11698176 | tf_op jit(solution)/shard_map/all_gather | solution.py:99
  9.3 377.9 %reduce-scatter.2.cloned.1.call-start = ((), (), s32[]{:S(2)}) async-start(), calls=%async_computation.5 | async-start | bytes 6881280 | tf_op jit(solution)/shard_map/reduce_scatter | solution.py:102
  9.4 33.6 %collective-permute-start = (bf16[512,1344]{0,1:T(8,128)(2,1)}, bf16[512,1344]{0,1:T(8,128)(2,1)S(1)}, u32[]{:S(2)}, u32[]{:S(2)}) collective-permute-start(bf16[512,1344]{0,1:T(8,128)(2,1)} %param.10), channel_id=1, source_target_pairs={{0,2},{2,4},{4,6},{6,0},{1,3},{3,5},{5,7},{7,1},{8,10},{10,12},{12... | collective-permute-start | bytes 4128776 | tf_op jit(solution)/shard_map/ppermute | solution.py:43
  43.0 31.6 %collective-permute-start.1 = (bf16[512,1344]{0,1:T(8,128)(2,1)S(1)}, bf16[512,1344]{0,1:T(8,128)(2,1)}, u32[]{:S(2)}, u32[]{:S(2)}) collective-permute-start(bf16[512,1344]{0,1:T(8,128)(2,1)S(1)} %collective-permute-done), channel_id=1, source_target_pairs={{0,2},{2,4},{4,6},{6,0},{1,3},{3,5},{5,7},{7,1},{8,10},{10,12},{12... | collective-permute-start | bytes 4128776 | tf_op jit(solution)/shard_map/ppermute | solution.py:43
  74.6 30.9 %collective-permute-start.2 = (bf16[512,1344]{0,1:T(8,128)(2,1)}, bf16[512,1344]{0,1:T(8,128)(2,1)}, u32[]{:S(2)}, u32[]{:S(2)}) collective-permute-start(bf16[512,1344]{0,1:T(8,128)(2,1)} %collective-permute-done.1), channel_id=1, source_target_pairs={{0,2},{2,4},{4,6},{6,0},{1,3},{3,5},{5,7},{7,1},{8,10},{10,12},{12... | collective-permute-start | bytes 4128776 | tf_op jit(solution)/shard_map/ppermute | solution.py:43
  111.5 6.1 %copy-start.4 = (f32[5376]{0:T(1024)S(1)}, f32[5376]{0:T(1024)}, u32[]{:S(2)}) copy-start(f32[5376]{0:T(1024)} %param.11) | copy-start | bytes 64516
  111.7 4.0 %copy-start.1 = (bf16[512,10752]{0,1:T(8,128)(2,1)}, bf16[512,10752]{0,1:T(8,128)(2,1)S(1)}, u32[]{:S(2)}) copy-start(bf16[512,10752]{0,1:T(8,128)(2,1)S(1)} %constant_dynamic-update-slice_fusion) | copy-start | bytes 33030148
  117.6 9.0 %copy-start.2 = (f32[128]{0:T(128)S(1)}, f32[128]{0:T(128)}, u32[]{:S(2)}) copy-start(f32[128]{0:T(128)} %param.16) | copy-start | bytes 1540
  127.7 25.8 %collective-permute-start.5 = (bf16[512,4,128]{2,0,1:T(8,128)(2,1)S(1)}, bf16[512,4,128]{2,0,1:T(8,128)(2,1)S(1)}, u32[]{:S(2)}, u32[]{:S(2)}) collective-permute-start(bf16[512,4,128]{2,0,1:T(8,128)(2,1)S(1)} %pad_maximum_fusion), channel_id=1, source_target_pairs={{0,16},{8,24},{16,32},{24,40},{32,48},{40,56},{48,64},{56,72},{64,... | collective-permute-start | bytes 1572872 | tf_op jit(solution)/shard_map/ppermute | solution.py:15
  132.1 26.6 %collective-permute-start.6 = (bf16[512,4,128]{2,0,1:T(8,128)(2,1)S(1)}, bf16[512,4,128]{2,0,1:T(8,128)(2,1)S(1)}, u32[]{:S(2)}, u32[]{:S(2)}) collective-permute-start(bf16[512,4,128]{2,0,1:T(8,128)(2,1)S(1)} %pad_maximum_fusion), channel_id=1, source_target_pairs={{0,8},{8,16},{16,24},{24,32},{32,40},{40,48},{48,56},{56,64},{64,7... | collective-permute-start | bytes 1572872 | tf_op jit(solution)/shard_map/ppermute | solution.py:15
  143.7 30.0 %collective-permute-start.3 = (bf16[512,4,128]{0,2,1:T(8,128)(2,1)}, bf16[512,4,128]{0,2,1:T(8,128)(2,1)}, u32[]{:S(2)}, u32[]{:S(2)}) collective-permute-start(bf16[512,4,128]{0,2,1:T(8,128)(2,1)} %bitcast), channel_id=1, source_target_pairs={{0,16},{8,24},{16,32},{24,40},{32,48},{40,56},{48,64},{56,72},{64,... | collective-permute-start | bytes 1572872 | tf_op jit(solution)/shard_map/ppermute | solution.py:15
  149.5 35.4 %collective-permute-start.4 = (bf16[512,4,128]{0,2,1:T(8,128)(2,1)}, bf16[512,4,128]{0,2,1:T(8,128)(2,1)}, u32[]{:S(2)}, u32[]{:S(2)}) collective-permute-start(bf16[512,4,128]{0,2,1:T(8,128)(2,1)} %bitcast), channel_id=1, source_target_pairs={{0,8},{8,16},{16,24},{24,32},{32,40},{40,48},{48,56},{56,64},{64,7... | collective-permute-start | bytes 1572872 | tf_op jit(solution)/shard_map/ppermute | solution.py:15
  247.3 1.4 copy-start.3
Sparse Core Ops, SparseCore 0:
  9.5 61.0 all-gather.6
  72.7 57.3 all-gather.4
  132.2 103.2 all-gather.8
  237.5 81.8 all-gather.10
  330.1 57.1 reduce-scatter.1
